TPU v7x, 128 devices: a whole 4x4x4 slice. The times are simulated.
128 devices in a mesh: ctx: 16 (over z_lo, y, core), ch: 8 (over z_hi, x).
Axes of the slice: x: 4, y: 4, z: 4 (z_hi: 2, z_lo: 2; z = z_hi * 2 + z_lo), core: 2. Of those that a mesh axis runs over, the one named last changes fastest.
Arguments:
- q_vals: bfloat16 [8192, 4096], P('ch', 'ctx'), may hold values from -6 to 6
- k_vals: bfloat16 [8192, 4096], P('ch', 'ctx'), may hold values from -6 to 6
- v_vals: bfloat16 [8192, 4096], P('ch', 'ctx'), may hold values from -6 to 6
- grad_out: bfloat16 [8192, 4096], P('ch', 'ctx'), may hold values from -6 to 6
- exponents: int32 [3, 64, 32], P(None, 'ch', 'ctx'), may hold values from -2 to 1
- filter_taps: float32 [512, 1024], P('ch'), may hold values from -1 to 1
Outputs:
- grad_q: bfloat16 [8192, 4096], P('ch', 'ctx')
- grad_k: bfloat16 [8192, 4096], P('ch', 'ctx')
- grad_v: bfloat16 [8192, 4096], P('ch', 'ctx')
- grad_filter: float32 [512, 1024], P('ch', 'ctx')
- grad_amax: float32 [3, 32], P(None, 'ctx')
All inputs are finite; a program needn't handle non-finite values.
Results may differ from a plain program's by a relative error of at most 0.0061.
Values may be sent and summed in bfloat16 or wider, within the bound.
No kernel may reach another device: no remote copies, remote signals or barrier semaphores. Data moves between devices by JAX's collectives and lax.ppermute only.
A program may use at most 128 MiB of HBM per device.

v0:
```python
import functools

import jax
import jax.numpy as jnp
from jax import lax
from jax.experimental import pallas as pl
from jax.experimental.pallas import tpu as pltpu
from jax.sharding import PartitionSpec as P

WINDOW = 4
EPS = 1e-06
TILE = 128


def shift_by(shard, axis, by):
    devices = lax.axis_size(axis)
    return lax.ppermute(shard, axis, [(i, (i + by) % devices) for i in range(devices)])


def power(exponent):
    return lax.shift_left(jnp.int32(1), exponent + 8).astype(jnp.float32) * (2.0 ** -8)


def gate_kernel(e_ref, q_ref, k_ref, v_ref, g_ref, z_ref, gw_ref):
    b = pl.program_id(0)
    for r in range(q_ref.shape[1] // TILE):
        lanes = slice(r * TILE, (r + 1) * TILE)
        q_real = q_ref[:, lanes].astype(jnp.float32) * power(e_ref[0, b, r])
        k_real = k_ref[:, lanes].astype(jnp.float32) * power(e_ref[1, b, r])
        v_real = v_ref[:, lanes].astype(jnp.float32) * power(e_ref[2, b, r])
        z_ref[:, lanes] = (k_real * v_real).astype(jnp.bfloat16)
        gw_ref[:, lanes] = (q_real * g_ref[:, lanes].astype(jnp.float32)).astype(jnp.bfloat16)


def conv_kernel(e_ref, taps_ref, *refs, width, halo):
    zs = refs[: halo + 1]
    gws = refs[halo + 1 : 2 * halo + 2]
    k_ref, v_ref, g_ref, w_ref, gz_ref, lag_ref, peak_ref, toe_ref, corr_ref = refs[2 * halo + 2 :]
    b = pl.program_id(0)
    groups, taps = taps_ref.shape
    rows = w_ref.shape[1]
    parts = rows // TILE
    span = taps + TILE
    tiles = span // TILE

    @pl.when(b == 0)
    def _():
        peak_ref[...] = jnp.zeros(peak_ref.shape, jnp.float32)

    def one_group(g, carry):
        at = pl.ds(pl.multiple_of(g * width, width), width)
        row = taps_ref[pl.ds(g, 1), :].astype(jnp.bfloat16).astype(jnp.float32)
        row = jnp.concatenate([row, jnp.zeros((1, TILE), jnp.float32)], axis=1)
        base = pltpu.roll(jnp.broadcast_to(row, (8, span)), 0, 1, stride=1, stride_axis=0)
        for a in range(0, TILE, 16):
            low = pltpu.roll(base, a, 1) if a else base
            high = pltpu.roll(base, a + 8, 1)
            toe_ref[a : a + 16, :] = jnp.concatenate([low, high], axis=0).astype(jnp.bfloat16)
        z_all = jnp.concatenate([ref[at, :] for ref in reversed(zs)], axis=1)
        gw_all = jnp.concatenate([ref[at, :] for ref in gws], axis=1)
        z_win = jnp.concatenate(
            [
                jnp.concatenate(
                    [z_all[:, (p + tiles - 1 - d) * TILE : (p + tiles - d) * TILE] for d in range(tiles)],
                    axis=1,
                )
                for p in range(parts)
            ],
            axis=0,
        )
        gw_win = jnp.concatenate(
            [gw_all[:, p * TILE : p * TILE + span] for p in range(parts)], axis=0
        )
        stacked = jnp.concatenate(
            [toe_ref[:, d * TILE : (d + 1) * TILE] for d in range(tiles)], axis=0
        )
        w = jnp.dot(z_win, stacked, preferred_element_type=jnp.float32)
        gz = lax.dot_general(
            gw_win, toe_ref[...], (((1,), (1,)), ((), ())), preferred_element_type=jnp.float32
        )
        z_own = z_all[:, taps : taps + rows]
        z_loc = jnp.concatenate([z_own[:, p * TILE : (p + 1) * TILE] for p in range(parts)], axis=0)
        corr_ref[...] = lax.dot_general(
            z_loc, gw_win, (((0,), (0,)), ((), ())), preferred_element_type=jnp.float32
        )
        fold = TILE // 2
        held = corr_ref[0:fold, :] + pltpu.roll(corr_ref[fold : 2 * fold, :], span - fold, 1)
        while fold > 1:
            fold //= 2
            held = held[0:fold, :] + pltpu.roll(held[fold : 2 * fold, :], span - fold, 1)
        lag_ref[pl.ds(g, 1), :] = held[:, :taps]
        for p in range(parts):
            lanes = slice(p * TILE, (p + 1) * TILE)
            w_p = w[p * width : (p + 1) * width, :]
            gz_p = gz[p * width : (p + 1) * width, :]
            w_ref[at, lanes] = w_p
            gz_ref[at, lanes] = gz_p
            products = (
                g_ref[at, lanes].astype(jnp.float32) * w_p,
                gz_p * (v_ref[at, lanes].astype(jnp.float32) * power(e_ref[2, b, p])),
                gz_p * (k_ref[at, lanes].astype(jnp.float32) * power(e_ref[1, b, p])),
            )
            for i, product in enumerate(products):
                top = jnp.max(jnp.abs(product), axis=0, keepdims=True)
                spot = slice(p * 4 + i, p * 4 + i + 1)
                peak_ref[spot, :] = jnp.maximum(peak_ref[spot, :], top)
        return carry

    lax.fori_loop(0, groups, one_group, 0)


def scale_kernel(e_ref, peak_ref, k_ref, v_ref, g_ref, w_ref, gz_ref, oq_ref, ok_ref, ov_ref):
    b = pl.program_id(0)
    for p in range(w_ref.shape[1] // TILE):
        lanes = slice(p * TILE, (p + 1) * TILE)
        inverse = 1.0 / (peak_ref[...] + EPS)
        w = w_ref[:, lanes]
        gz = gz_ref[:, lanes]
        oq_ref[:, lanes] = (
            g_ref[:, lanes].astype(jnp.float32) * w * inverse[p * 4 : p * 4 + 1, :]
        ).astype(jnp.bfloat16)
        v_real = v_ref[:, lanes].astype(jnp.float32) * power(e_ref[2, b, p])
        k_real = k_ref[:, lanes].astype(jnp.float32) * power(e_ref[1, b, p])
        ok_ref[:, lanes] = (gz * v_real * inverse[p * 4 + 1 : p * 4 + 2, :]).astype(jnp.bfloat16)
        ov_ref[:, lanes] = (gz * k_real * inverse[p * 4 + 2 : p * 4 + 3, :]).astype(jnp.bfloat16)


def shards(q_vals, k_vals, v_vals, grad_out, exponents, filter_taps):
    channels, rows = q_vals.shape
    groups, taps = filter_taps.shape
    blocks = exponents.shape[1]
    block = channels // blocks
    width = channels // groups
    halo = taps // rows
    steps = (blocks,)
    scalars = pl.BlockSpec(memory_space=pltpu.SMEM)
    tile = pl.BlockSpec((block, rows), lambda b: (b, 0))
    whole = pl.BlockSpec((8, TILE), lambda b: (0, 0))
    shape = lambda dtype: jax.ShapeDtypeStruct((channels, rows), dtype)

    z, gw = pl.pallas_call(
        gate_kernel,
        grid=steps,
        in_specs=[scalars] + [tile] * 4,
        out_specs=[tile] * 2,
        out_shape=[shape(jnp.bfloat16)] * 2,
        name="gate",
    )(exponents, q_vals, k_vals, v_vals, grad_out)

    zs = [z]
    gws = [gw]
    for _ in range(halo):
        zs.append(shift_by(zs[-1], "ctx", 1))
        gws.append(shift_by(gws[-1], "ctx", -1))

    per_block = groups // blocks
    lag_block = pl.BlockSpec((per_block, taps), lambda b: (b, 0))
    w, gz, lag, peak = pl.pallas_call(
        functools.partial(conv_kernel, width=width, halo=halo),
        grid=steps,
        in_specs=[scalars, lag_block] + [tile] * (2 * halo + 2 + 3),
        out_specs=[tile, tile, lag_block, whole],
        out_shape=[
            shape(jnp.float32),
            shape(jnp.float32),
            jax.ShapeDtypeStruct((groups, taps), jnp.float32),
            jax.ShapeDtypeStruct((8, TILE), jnp.float32),
        ],
        scratch_shapes=[
            pltpu.VMEM((TILE, taps + TILE), jnp.bfloat16),
            pltpu.VMEM((TILE, taps + TILE), jnp.float32),
        ],
        name="conv",
    )(exponents, filter_taps, *zs, *gws, k_vals, v_vals, grad_out)

    ch = lax.axis_size("ch")
    peak_all = lax.all_to_all(
        jnp.broadcast_to(peak, (ch, 8, TILE)), "ch", split_axis=0, concat_axis=0, tiled=True
    )
    peak = jnp.broadcast_to(jnp.max(peak_all, axis=(0, 2))[:, None], (8, TILE))

    oq, ok, ov = pl.pallas_call(
        scale_kernel,
        grid=steps,
        in_specs=[scalars, whole] + [tile] * 5,
        out_specs=[tile] * 3,
        out_shape=[shape(jnp.bfloat16)] * 3,
        name="scale",
    )(exponents, peak, k_vals, v_vals, grad_out, w, gz)

    ctx = lax.axis_size("ctx")
    pieces = lax.all_to_all(
        lag.reshape(groups, ctx, taps // ctx).transpose(1, 0, 2), "ctx", split_axis=0, concat_axis=0, tiled=True
    )
    grad_filter = jnp.sum(pieces, axis=0)
    block_peak = peak[:, 0].reshape(2, 4)[:, :3].T
    return oq, ok, ov, grad_filter, block_peak


def solution(mesh):
    in_specs = (
        P("ch", "ctx"),
        P("ch", "ctx"),
        P("ch", "ctx"),
        P("ch", "ctx"),
        P(None, "ch", "ctx"),
        P("ch", None),
    )
    out_specs = (P("ch", "ctx"), P("ch", "ctx"), P("ch", "ctx"), P("ch", "ctx"), P(None, "ctx"))
    return jax.shard_map(shards, mesh=mesh, in_specs=in_specs, out_specs=out_specs, check_vma=False)
```

profile of v0, /device:TPU:0, one launch (start us, length us, event | category | flops | bytes accessed | tf_op | source)
XLA Modules:
  0.0 153.7 jit_solution(15528181127658666408)
XLA Ops:
  0.6 1.4 copy.20.e_ref
  2.0 5.6 %gate.1 = (bf16[1024,256]{1,0:T(8,128)(2,1)}, bf16[1024,256]{1,0:T(8,128)(2,1)}) custom-call(s32[3,8,2]{2,1,0:T(8,128)} %copy.20.e_ref, bf16[1024,256]{1,0:T(8,128)(2,1)} %q_ref.1, bf16[1024,256]{1,0:T(8,128)(2,1)} %k_ref.3, bf16[1024,256]{1,0:T(8,128)(2,1)} %v_ref.3, bf16[1024,256]{1,0:T(8,128)(2,1)} %g_ref.3), custom_call_target="tpu_custom_call" | custom-call | tf_op jit(solution)/shard_map/gate/pallas_call | solution.py:141
  7.6 0.0 collective-permute-start
  7.6 4.0 %collective-permute-start.4 = (bf16[1024,256]{1,0:T(8,128)(2,1)}, bf16[1024,256]{1,0:T(8,128)(2,1)S(1)}, u32[]{:S(2)}, u32[]{:S(2)}) collective-permute-start(bf16[1024,256]{1,0:T(8,128)(2,1)} %get-tuple-element.15.refs_5_), channel_id=1, source_target_pairs={{0,120},{8,0},{16,8},{24,16},{32,24},{40,32},{48,40},{56,48},{64,5... | collective-permute-start | bytes 1572872 | tf_op jit(solution)/shard_map/ppermute | solution.py:17
  11.5 7.0 %collective-permute-done.refs_1_ = bf16[1024,256]{1,0:T(8,128)(2,1)S(1)} collective-permute-done((bf16[1024,256]{1,0:T(8,128)(2,1)}, bf16[1024,256]{1,0:T(8,128)(2,1)S(1)}, u32[]{:S(2)}, u32[]{:S(2)}) %collective-permute-start) | collective-permute-done | bytes 524320 | tf_op jit(solution)/shard_map/ppermute | solution.py:17
  18.5 0.0 copy-start
  18.5 0.0 collective-permute-start.1
  18.5 0.0 collective-permute-done.4.refs_6_
  18.5 0.0 copy-start.1
  18.5 3.9 %collective-permute-start.5 = (bf16[1024,256]{1,0:T(8,128)(2,1)S(1)}, bf16[1024,256]{1,0:T(8,128)(2,1)S(1)}, u32[]{:S(2)}, u32[]{:S(2)}) collective-permute-start(bf16[1024,256]{1,0:T(8,128)(2,1)S(1)} %collective-permute-done.4.refs_6_), channel_id=1, source_target_pairs={{0,120},{8,0},{16,8},{24,16},{32,24},{40,32},{48,40},{56,48},{64,5... | collective-permute-start | bytes 1572872 | tf_op jit(solution)/shard_map/ppermute | solution.py:17
  22.4 6.8 %collective-permute-done.1.refs_2_ = bf16[1024,256]{1,0:T(8,128)(2,1)S(1)} collective-permute-done((bf16[1024,256]{1,0:T(8,128)(2,1)S(1)}, bf16[1024,256]{1,0:T(8,128)(2,1)S(1)}, u32[]{:S(2)}, u32[]{:S(2)}) %collective-permute-start.1) | collective-permute-done | bytes 524320 | tf_op jit(solution)/shard_map/ppermute | solution.py:17
  29.2 0.0 copy-start.2
  29.2 0.0 collective-permute-start.2
  29.2 0.0 collective-permute-done.5.refs_7_
  29.2 0.0 copy-start.3
  29.3 3.9 %collective-permute-start.6 = (bf16[1024,256]{1,0:T(8,128)(2,1)S(1)}, bf16[1024,256]{1,0:T(8,128)(2,1)S(1)}, u32[]{:S(2)}, u32[]{:S(2)}) collective-permute-start(bf16[1024,256]{1,0:T(8,128)(2,1)S(1)} %collective-permute-done.5.refs_7_), channel_id=1, source_target_pairs={{0,120},{8,0},{16,8},{24,16},{32,24},{40,32},{48,40},{56,48},{64,5... | collective-permute-start | bytes 1572872 | tf_op jit(solution)/shard_map/ppermute | solution.py:17
  33.2 6.8 %collective-permute-done.2.refs_3_ = bf16[1024,256]{1,0:T(8,128)(2,1)S(1)} collective-permute-done((bf16[1024,256]{1,0:T(8,128)(2,1)S(1)}, bf16[1024,256]{1,0:T(8,128)(2,1)S(1)}, u32[]{:S(2)}, u32[]{:S(2)}) %collective-permute-start.2) | collective-permute-done | bytes 524320 | tf_op jit(solution)/shard_map/ppermute | solution.py:17
  40.0 0.0 copy-start.4
  40.0 0.0 collective-permute-start.3
  40.0 0.0 collective-permute-done.6.refs_8_
  40.0 0.0 copy-start.5
  40.0 3.9 %collective-permute-start.7 = (bf16[1024,256]{1,0:T(8,128)(2,1)S(1)}, bf16[1024,256]{1,0:T(8,128)(2,1)}, u32[]{:S(2)}, u32[]{:S(2)}) collective-permute-start(bf16[1024,256]{1,0:T(8,128)(2,1)S(1)} %collective-permute-done.6.refs_8_), channel_id=1, source_target_pairs={{0,120},{8,0},{16,8},{24,16},{32,24},{40,32},{48,40},{56,48},{64,5... | collective-permute-start | bytes 1572872 | tf_op jit(solution)/shard_map/ppermute | solution.py:17
  43.9 6.8 %collective-permute-done.3.refs_4_ = bf16[1024,256]{1,0:T(8,128)(2,1)S(1)} collective-permute-done((bf16[1024,256]{1,0:T(8,128)(2,1)S(1)}, bf16[1024,256]{1,0:T(8,128)(2,1)S(1)}, u32[]{:S(2)}, u32[]{:S(2)}) %collective-permute-start.3) | collective-permute-done | bytes 524320 | tf_op jit(solution)/shard_map/ppermute | solution.py:17
  50.7 0.0 copy-start.6
  50.7 0.8 copy-done.6
  51.5 0.0 collective-permute-done.7.refs_9_
  51.5 0.0 copy-done
  51.5 0.0 copy-done.1
  51.5 0.0 copy-done.2
  51.5 0.0 copy-done.3
  51.5 0.0 copy-done.4
  51.5 0.0 copy-done.5
  51.5 71.4 %conv.1 = (f32[1024,256]{1,0:T(8,128)}, f32[1024,256]{1,0:T(8,128)}, f32[64,1024]{1,0:T(8,128)}, f32[8,128]{1,0:T(8,128)}) custom-call(s32[3,8,2]{2,1,0:T(8,128)} %copy.20.e_ref, f32[64,1024]{1,0:T(8,128)} %taps_ref.1, bf16[1024,256]{1,0:T(8,128)(2,1)} %get-tuple-element.14.refs_0_, bf16[1024,256]{1,0:T(8,128)(2,1)} %copy-done, bf16[1024,256]{1,0:T(8,128)(2,1)} %copy-done.2, ...), custom_call_target="tpu_custom_call" | custom-call | tf_op jit(solution)/shard_map/conv/pallas_call | solution.py:158
  122.9 1.3 broadcast_in_dim.4
  124.2 7.7 %all-to-all-start = ((f32[8,8,128]{2,1,0:T(8,128)}), f32[8,8,128]{2,1,0:T(8,128)S(1)}, u32[]{:S(2)}, u32[]{:S(2)}) async-start(f32[8,8,128]{2,1,0:T(8,128)} %broadcast_in_dim.4), calls=%async_computation | async-start | bytes 65536 | tf_op jit(solution)/shard_map/all_to_all | solution.py:177
  131.9 1.1 reshape.15
  133.0 0.2 copy.23
  133.1 1.0 reshape.16
  134.2 5.5 %all-to-all-done = f32[8,8,128]{2,1,0:T(8,128)S(1)} async-done(((f32[8,8,128]{2,1,0:T(8,128)}), f32[8,8,128]{2,1,0:T(8,128)S(1)}, u32[]{:S(2)}, u32[]{:S(2)}) %all-to-all-start) | async-done | bytes 32800 | tf_op jit(solution)/shard_map/all_to_all | solution.py:177
  139.6 3.5 %all-to-all-start.1 = ((f32[16,1,4096]{2,1,0:T(1,128)}), f32[16,1,4096]{2,1,0:T(1,128)S(1)}, u32[]{:S(2)}, u32[]{:S(2)}) async-start(f32[16,1,4096]{2,1,0:T(1,128)} %reshape.16), calls=%async_computation.1 | async-start | bytes 524288 | tf_op jit(solution)/shard_map/all_to_all | solution.py:192
  143.2 0.1 reduce_max.9
  143.3 0.1 slice.6
  143.4 0.7 broadcast_in_dim.10.peak_ref
  144.0 6.0 %scale.1 = (bf16[1024,256]{1,0:T(8,128)(2,1)}, bf16[1024,256]{1,0:T(8,128)(2,1)}, bf16[1024,256]{1,0:T(8,128)(2,1)}) custom-call(s32[3,8,2]{2,1,0:T(8,128)} %copy.20.e_ref, f32[8,128]{1,0:T(8,128)} %broadcast_in_dim.10.peak_ref, bf16[1024,256]{1,0:T(8,128)(2,1)} %k_ref.3, bf16[1024,256]{1,0:T(8,128)(2,1)} %v_ref.3, bf16[1024,256]{1,0:T(8,128)(2,1)} %g_ref.3, ...), custom_call_target="tpu_custom_call" | custom-call | tf_op jit(solution)/shard_map/scale/pallas_call | solution.py:182
  150.1 0.6 slice_bitcast_fusion
  150.6 0.4 all-to-all-done.1
  151.0 0.5 broadcast.2
  151.5 1.3 reduce
  152.8 0.2 reshape.17
  153.0 0.7 reduce_sum.9
Async XLA Ops:
  7.6 11.0 %collective-permute-start = (bf16[1024,256]{1,0:T(8,128)(2,1)}, bf16[1024,256]{1,0:T(8,128)(2,1)S(1)}, u32[]{:S(2)}, u32[]{:S(2)}) collective-permute-start(bf16[1024,256]{1,0:T(8,128)(2,1)} %get-tuple-element.14.refs_0_), channel_id=1, source_target_pairs={{0,8},{8,16},{16,24},{24,32},{32,40},{40,48},{48,56},{56,64},{64,7... | collective-permute-start | bytes 1572872 | tf_op jit(solution)/shard_map/ppermute | solution.py:17
  7.6 11.0 %collective-permute-start.4 = (bf16[1024,256]{1,0:T(8,128)(2,1)}, bf16[1024,256]{1,0:T(8,128)(2,1)S(1)}, u32[]{:S(2)}, u32[]{:S(2)}) collective-permute-start(bf16[1024,256]{1,0:T(8,128)(2,1)} %get-tuple-element.15.refs_5_), channel_id=1, source_target_pairs={{0,120},{8,0},{16,8},{24,16},{32,24},{40,32},{48,40},{56,48},{64,5... | collective-permute-start | bytes 1572872 | tf_op jit(solution)/shard_map/ppermute | solution.py:17
  18.5 33.0 %copy-start = (bf16[1024,256]{1,0:T(8,128)(2,1)}, bf16[1024,256]{1,0:T(8,128)(2,1)S(1)}, u32[]{:S(2)}) copy-start(bf16[1024,256]{1,0:T(8,128)(2,1)S(1)} %collective-permute-done.refs_1_) | copy-start | bytes 1572868
  18.5 10.7 %collective-permute-start.1 = (bf16[1024,256]{1,0:T(8,128)(2,1)S(1)}, bf16[1024,256]{1,0:T(8,128)(2,1)S(1)}, u32[]{:S(2)}, u32[]{:S(2)}) collective-permute-start(bf16[1024,256]{1,0:T(8,128)(2,1)S(1)} %collective-permute-done.refs_1_), channel_id=1, source_target_pairs={{0,8},{8,16},{16,24},{24,32},{32,40},{40,48},{48,56},{56,64},{64,7... | collective-permute-start | bytes 1572872 | tf_op jit(solution)/shard_map/ppermute | solution.py:17
  18.5 33.0 %copy-start.1 = (bf16[1024,256]{1,0:T(8,128)(2,1)}, bf16[1024,256]{1,0:T(8,128)(2,1)S(1)}, u32[]{:S(2)}) copy-start(bf16[1024,256]{1,0:T(8,128)(2,1)S(1)} %collective-permute-done.4.refs_6_) | copy-start | bytes 1572868
  18.5 10.7 %collective-permute-start.5 = (bf16[1024,256]{1,0:T(8,128)(2,1)S(1)}, bf16[1024,256]{1,0:T(8,128)(2,1)S(1)}, u32[]{:S(2)}, u32[]{:S(2)}) collective-permute-start(bf16[1024,256]{1,0:T(8,128)(2,1)S(1)} %collective-permute-done.4.refs_6_), channel_id=1, source_target_pairs={{0,120},{8,0},{16,8},{24,16},{32,24},{40,32},{48,40},{56,48},{64,5... | collective-permute-start | bytes 1572872 | tf_op jit(solution)/shard_map/ppermute | solution.py:17
  29.2 22.3 %copy-start.2 = (bf16[1024,256]{1,0:T(8,128)(2,1)}, bf16[1024,256]{1,0:T(8,128)(2,1)S(1)}, u32[]{:S(2)}) copy-start(bf16[1024,256]{1,0:T(8,128)(2,1)S(1)} %collective-permute-done.1.refs_2_) | copy-start | bytes 1572868
  29.2 10.7 %collective-permute-start.2 = (bf16[1024,256]{1,0:T(8,128)(2,1)S(1)}, bf16[1024,256]{1,0:T(8,128)(2,1)S(1)}, u32[]{:S(2)}, u32[]{:S(2)}) collective-permute-start(bf16[1024,256]{1,0:T(8,128)(2,1)S(1)} %collective-permute-done.1.refs_2_), channel_id=1, source_target_pairs={{0,8},{8,16},{16,24},{24,32},{32,40},{40,48},{48,56},{56,64},{64,7... | collective-permute-start | bytes 1572872 | tf_op jit(solution)/shard_map/ppermute | solution.py:17
  29.2 22.3 %copy-start.3 = (bf16[1024,256]{1,0:T(8,128)(2,1)}, bf16[1024,256]{1,0:T(8,128)(2,1)S(1)}, u32[]{:S(2)}) copy-start(bf16[1024,256]{1,0:T(8,128)(2,1)S(1)} %collective-permute-done.5.refs_7_) | copy-start | bytes 1572868
  29.3 10.7 %collective-permute-start.6 = (bf16[1024,256]{1,0:T(8,128)(2,1)S(1)}, bf16[1024,256]{1,0:T(8,128)(2,1)S(1)}, u32[]{:S(2)}, u32[]{:S(2)}) collective-permute-start(bf16[1024,256]{1,0:T(8,128)(2,1)S(1)} %collective-permute-done.5.refs_7_), channel_id=1, source_target_pairs={{0,120},{8,0},{16,8},{24,16},{32,24},{40,32},{48,40},{56,48},{64,5... | collective-permute-start | bytes 1572872 | tf_op jit(solution)/shard_map/ppermute | solution.py:17
  40.0 11.6 %copy-start.4 = (bf16[1024,256]{1,0:T(8,128)(2,1)}, bf16[1024,256]{1,0:T(8,128)(2,1)S(1)}, u32[]{:S(2)}) copy-start(bf16[1024,256]{1,0:T(8,128)(2,1)S(1)} %collective-permute-done.2.refs_3_) | copy-start | bytes 1572868
  40.0 10.7 %collective-permute-start.3 = (bf16[1024,256]{1,0:T(8,128)(2,1)S(1)}, bf16[1024,256]{1,0:T(8,128)(2,1)S(1)}, u32[]{:S(2)}, u32[]{:S(2)}) collective-permute-start(bf16[1024,256]{1,0:T(8,128)(2,1)S(1)} %collective-permute-done.2.refs_3_), channel_id=1, source_target_pairs={{0,8},{8,16},{16,24},{24,32},{32,40},{40,48},{48,56},{56,64},{64,7... | collective-permute-start | bytes 1572872 | tf_op jit(solution)/shard_map/ppermute | solution.py:17
  40.0 11.6 %copy-start.5 = (bf16[1024,256]{1,0:T(8,128)(2,1)}, bf16[1024,256]{1,0:T(8,128)(2,1)S(1)}, u32[]{:S(2)}) copy-start(bf16[1024,256]{1,0:T(8,128)(2,1)S(1)} %collective-permute-done.6.refs_8_) | copy-start | bytes 1572868
  40.0 11.5 %collective-permute-start.7 = (bf16[1024,256]{1,0:T(8,128)(2,1)S(1)}, bf16[1024,256]{1,0:T(8,128)(2,1)}, u32[]{:S(2)}, u32[]{:S(2)}) collective-permute-start(bf16[1024,256]{1,0:T(8,128)(2,1)S(1)} %collective-permute-done.6.refs_8_), channel_id=1, source_target_pairs={{0,120},{8,0},{16,8},{24,16},{32,24},{40,32},{48,40},{56,48},{64,5... | collective-permute-start | bytes 1572872 | tf_op jit(solution)/shard_map/ppermute | solution.py:17
  50.7 0.8 copy-start.6
  124.2 15.4 %all-to-all-start = ((f32[8,8,128]{2,1,0:T(8,128)}), f32[8,8,128]{2,1,0:T(8,128)S(1)}, u32[]{:S(2)}, u32[]{:S(2)}) async-start(f32[8,8,128]{2,1,0:T(8,128)} %broadcast_in_dim.4), calls=%async_computation | async-start | bytes 65536 | tf_op jit(solution)/shard_map/all_to_all | solution.py:177
  139.6 11.4 %all-to-all-start.1 = ((f32[16,1,4096]{2,1,0:T(1,128)}), f32[16,1,4096]{2,1,0:T(1,128)S(1)}, u32[]{:S(2)}, u32[]{:S(2)}) async-start(f32[16,1,4096]{2,1,0:T(1,128)} %reshape.16), calls=%async_computation.1 | async-start | bytes 524288 | tf_op jit(solution)/shard_map/all_to_all | solution.py:192
where the time goes:
time: 155 us; the launch traced here: 154 us
  Pallas kernels  82.9 us (53%)
  waiting for transfers between devices  33.3 us (21%)
  starting transfers between devices  26.9 us (17%)
  local copies, waits for them, and re-layouts  7.8 us (5%)
  other arithmetic  2.05 us (1%)
    pallas_call x1, Pallas kernels, shards(): pl.pallas_call(functools.partial(conv_kernel, width=width, halo=halo), gr...  71.4 us
    ppermute x8, waiting for transfers between devices, shift_by(): lax.ppermute(shard, axis, [(i, (i + by) % devices) for i in range(devices)])  27.4 us
    ppermute x8, starting transfers between devices, shift_by(): lax.ppermute(shard, axis, [(i, (i + by) % devices) for i in range(devices)])  15.7 us
    all_to_all x1, starting transfers between devices, shards(): lax.all_to_all(jnp.broadcast_to(peak, (ch, 8, TILE)), 'ch', split_axis=0,...  7.66 us
    pallas_call x1, Pallas kernels, shards(): pl.pallas_call(scale_kernel, grid=steps, in_specs=[scalars, whole] + [til...  6.01 us
    pallas_call x1, Pallas kernels, shards(): pl.pallas_call(gate_kernel, grid=steps, in_specs=[scalars] + [tile] * 4,...  5.56 us
    all_to_all x1, waiting for transfers between devices, shards(): lax.all_to_all(jnp.broadcast_to(peak, (ch, 8, TILE)), 'ch', split_axis=0,...  5.47 us
    all_to_all x1, starting transfers between devices, shards(): lax.all_to_all(lag.reshape(groups, ctx, taps // ctx).transpose(1, 0, 2),...  3.53 us
  transfers between devices with their start and end apart: 10, of which 6 were waited for; matrix products, arithmetic and copies ran while one was open for 2% of the time, Pallas kernels for 4%

commit v1 on v0

v1 whole, which is shorter than its diff:
```python
import functools

import jax
import jax.numpy as jnp
from jax import lax
from jax.experimental import pallas as pl
from jax.experimental.pallas import tpu as pltpu
from jax.sharding import PartitionSpec as P

WINDOW = 4
EPS = 1e-06
TILE = 128
FINE = 32
UNROLL = 4


def shift_by(shard, axis, by):
    devices = lax.axis_size(axis)
    return lax.ppermute(shard, axis, [(i, (i + by) % devices) for i in range(devices)])


def power(exponent):
    return lax.shift_left(jnp.int32(1), exponent + 8).astype(jnp.float32) * (2.0 ** -8)


def mirror():
    shape = (TILE, TILE)
    rows = lax.broadcasted_iota(jnp.int32, shape, 0)
    lanes = lax.broadcasted_iota(jnp.int32, shape, 1)
    return (rows + lanes == TILE - 1).astype(jnp.float32).astype(jnp.bfloat16)


def mirrored(values, flip, terms):
    pieces = []
    rest = values
    for _ in range(terms):
        piece = rest.astype(jnp.bfloat16)
        pieces.append(piece)
        rest = rest - piece.astype(jnp.float32)
    return jnp.dot(
        jnp.concatenate(pieces, axis=1),
        jnp.concatenate([flip] * terms, axis=0),
        preferred_element_type=jnp.float32,
    )


def gate_kernel(e_ref, q_ref, k_ref, v_ref, g_ref, z_ref, back_ref):
    b = pl.program_id(0)
    flip = mirror()
    parts = q_ref.shape[1] // TILE
    for r in range(parts):
        lanes = slice(r * TILE, (r + 1) * TILE)
        other = slice((parts - 1 - r) * TILE, (parts - r) * TILE)
        q_real = q_ref[:, lanes].astype(jnp.float32) * power(e_ref[0, b, r])
        k_real = k_ref[:, lanes].astype(jnp.float32) * power(e_ref[1, b, r])
        v_real = v_ref[:, lanes].astype(jnp.float32) * power(e_ref[2, b, r])
        z_ref[:, lanes] = (k_real * v_real).astype(jnp.bfloat16)
        gw = (q_real * g_ref[:, lanes].astype(jnp.float32)).astype(jnp.bfloat16)
        back_ref[:, other] = jnp.dot(gw, flip, preferred_element_type=jnp.float32).astype(jnp.bfloat16)


def conv_kernel(e_ref, taps_ref, *refs, width, halo, first):
    zs = refs[: halo + 1]
    backs = refs[halo + 1 : 2 * halo + 2]
    k_ref, v_ref, g_ref, w_ref, gz_ref, lag_ref, peak_ref, turn_ref, diag_ref, *toe_refs = refs[2 * halo + 2 :]
    step = pl.program_id(0)
    b = step + first
    groups, taps = taps_ref.shape
    rows = w_ref.shape[1]
    parts = rows // TILE
    span = taps + TILE
    tiles = span // TILE

    @pl.when(step == 0)
    def _():
        peak_ref[...] = jnp.zeros(peak_ref.shape, jnp.float32)

    def windows(everything):
        return [
            jnp.concatenate(
                [
                    everything[:, (p + tiles - 1 - d) * TILE : (p + tiles - d) * TILE]
                    for d in range(tiles)
                ],
                axis=1,
            )
            for p in range(parts)
        ]

    def one_group(g, toe_ref):
        at = pl.ds(pl.multiple_of(g * width, width), width)
        row = taps_ref[pl.ds(g, 1), :].astype(jnp.bfloat16).astype(jnp.float32)
        row = jnp.concatenate([row, jnp.zeros((1, TILE), jnp.float32)], axis=1)
        row = jnp.broadcast_to(row, (8, span))
        low = pltpu.roll(row, 0, 1, stride=1, stride_axis=0)
        high = pltpu.roll(row, 8, 1, stride=1, stride_axis=0)
        base = jnp.concatenate([low, high], axis=0).astype(jnp.bfloat16)
        for a in range(0, TILE, 16):
            rolled = pltpu.roll(base, a, 1) if a else base
            for d in range(tiles):
                toe_ref[d * TILE + a : d * TILE + a + 16, :] = rolled[:, d * TILE : (d + 1) * TILE]
        z_all = jnp.concatenate([ref[at, :] for ref in reversed(zs)], axis=1)
        back_all = jnp.concatenate([ref[at, :] for ref in reversed(backs)], axis=1)
        sources = jnp.concatenate(windows(z_all) + windows(back_all), axis=0)
        both = jnp.dot(sources, toe_ref[...], preferred_element_type=jnp.float32)
        for p in range(parts):
            lanes = slice(p * TILE, (p + 1) * TILE)
            w_ref[at, lanes] = both[p * width : (p + 1) * width, :]
            turn_ref[at, lanes] = both[(parts + p) * width : (parts + p + 1) * width, :]
        back_own = back_all[:, taps : taps + rows]
        own_parts = []
        z_parts = []
        for m in range(TILE // FINE):
            z_m = pltpu.roll(z_all, taps + rows - m * FINE, 1) if m else z_all
            n = TILE // FINE - 1 - m
            back_n = pltpu.roll(back_own, rows - n * FINE, 1) if n else back_own
            for p in range(parts):
                z_parts.append(z_m[:, p * TILE : p * TILE + span])
                o = parts - 1 - p
                own_parts.append(back_n[:, o * TILE : (o + 1) * TILE])
        cross = lax.dot_general(
            jnp.concatenate(own_parts, axis=0),
            jnp.concatenate(z_parts, axis=0),
            (((0,), (0,)), ((), ())),
            preferred_element_type=jnp.float32,
        )
        total = None
        for a in range(0, FINE, 8):
            turned = pltpu.roll(
                cross[a : a + 8, :], (a + span - FINE) % span, 1, stride=1, stride_axis=0
            )
            total = turned if total is None else total + turned
        diag_ref[pl.ds(g, 1), :] = jnp.sum(total, axis=0, keepdims=True)[:, :taps]

    def some_groups(n, carry):
        for u in range(UNROLL):
            one_group(n * UNROLL + u, toe_refs[u])
        return carry

    lax.fori_loop(0, groups // UNROLL, some_groups, 0)

    flip = mirror()
    diag = diag_ref[...]
    blocks = taps // TILE
    stacked = jnp.concatenate([diag[:, n * TILE : (n + 1) * TILE] for n in range(blocks)], axis=0)
    stacked = mirrored(stacked, flip, 3)
    for n in range(blocks):
        o = blocks - 1 - n
        lag_ref[:, o * TILE : (o + 1) * TILE] = stacked[n * groups : (n + 1) * groups, :]
    for p in range(parts):
        o = parts - 1 - p
        lanes = slice(p * TILE, (p + 1) * TILE)
        gz = mirrored(turn_ref[:, o * TILE : (o + 1) * TILE], flip, 3)
        gz_ref[:, lanes] = gz
        products = (
            g_ref[:, lanes].astype(jnp.float32) * w_ref[:, lanes],
            gz * (v_ref[:, lanes].astype(jnp.float32) * power(e_ref[2, b, p])),
            gz * (k_ref[:, lanes].astype(jnp.float32) * power(e_ref[1, b, p])),
        )
        for i, product in enumerate(products):
            top = jnp.max(jnp.abs(product), axis=0, keepdims=True)
            spot = slice(p * 4 + i, p * 4 + i + 1)
            peak_ref[spot, :] = jnp.maximum(peak_ref[spot, :], top)


def scale_kernel(e_ref, peak_ref, k_ref, v_ref, g_ref, w_ref, gz_ref, oq_ref, ok_ref, ov_ref):
    b = pl.program_id(0)
    for p in range(w_ref.shape[1] // TILE):
        lanes = slice(p * TILE, (p + 1) * TILE)
        inverse = 1.0 / (peak_ref[...] + EPS)
        w = w_ref[:, lanes]
        gz = gz_ref[:, lanes]
        oq_ref[:, lanes] = (
            g_ref[:, lanes].astype(jnp.float32) * w * inverse[p * 4 : p * 4 + 1, :]
        ).astype(jnp.bfloat16)
        v_real = v_ref[:, lanes].astype(jnp.float32) * power(e_ref[2, b, p])
        k_real = k_ref[:, lanes].astype(jnp.float32) * power(e_ref[1, b, p])
        ok_ref[:, lanes] = (gz * v_real * inverse[p * 4 + 1 : p * 4 + 2, :]).astype(jnp.bfloat16)
        ov_ref[:, lanes] = (gz * k_real * inverse[p * 4 + 2 : p * 4 + 3, :]).astype(jnp.bfloat16)


def shards(q_vals, k_vals, v_vals, grad_out, exponents, filter_taps):
    channels, rows = q_vals.shape
    groups, taps = filter_taps.shape
    blocks = exponents.shape[1]
    block = channels // blocks
    width = channels // groups
    halo = taps // rows
    steps = (blocks,)
    scalars = pl.BlockSpec(memory_space=pltpu.SMEM)
    tile = pl.BlockSpec((block, rows), lambda b: (b, 0))
    whole = pl.BlockSpec((8, TILE), lambda b: (0, 0))
    shape = lambda dtype: jax.ShapeDtypeStruct((channels, rows), dtype)

    z, back = pl.pallas_call(
        gate_kernel,
        grid=steps,
        in_specs=[scalars] + [tile] * 4,
        out_specs=[tile] * 2,
        out_shape=[shape(jnp.bfloat16)] * 2,
        name="gate",
    )(exponents, q_vals, k_vals, v_vals, grad_out)

    zs = [z]
    backs = [back]
    for _ in range(halo):
        zs.append(shift_by(zs[-1], "ctx", 1))
        backs.append(shift_by(backs[-1], "ctx", -1))

    per_block = groups // blocks
    lag_block = pl.BlockSpec((per_block, taps), lambda b: (b, 0))
    w, gz, lag, peak = pl.pallas_call(
        functools.partial(conv_kernel, width=width, halo=halo, first=0),
        grid=steps,
        in_specs=[scalars, lag_block] + [tile] * (2 * halo + 2 + 3),
        out_specs=[tile, tile, lag_block, whole],
        out_shape=[
            shape(jnp.float32),
            shape(jnp.float32),
            jax.ShapeDtypeStruct((groups, taps), jnp.float32),
            jax.ShapeDtypeStruct((8, TILE), jnp.float32),
        ],
        scratch_shapes=[
            pltpu.VMEM((block, rows), jnp.float32),
            pltpu.VMEM((per_block, taps), jnp.float32),
        ]
        + [pltpu.VMEM((taps + TILE, TILE), jnp.bfloat16)] * UNROLL,
        name="conv",
    )(exponents, filter_taps, *zs, *backs, k_vals, v_vals, grad_out)

    ch = lax.axis_size("ch")
    peak_all = lax.all_to_all(
        jnp.broadcast_to(peak, (ch, 8, TILE)), "ch", split_axis=0, concat_axis=0, tiled=True
    )
    peak = jnp.broadcast_to(jnp.max(peak_all, axis=(0, 2))[:, None], (8, TILE))

    oq, ok, ov = pl.pallas_call(
        scale_kernel,
        grid=steps,
        in_specs=[scalars, whole] + [tile] * 5,
        out_specs=[tile] * 3,
        out_shape=[shape(jnp.bfloat16)] * 3,
        name="scale",
    )(exponents, peak, k_vals, v_vals, grad_out, w, gz)

    ctx = lax.axis_size("ctx")
    pieces = lax.all_to_all(
        lag.reshape(groups, ctx, taps // ctx).transpose(1, 0, 2), "ctx", split_axis=0, concat_axis=0, tiled=True
    )
    grad_filter = jnp.sum(pieces, axis=0)
    block_peak = peak[:, 0].reshape(2, 4)[:, :3].T
    return oq, ok, ov, grad_filter, block_peak


def solution(mesh):
    in_specs = (
        P("ch", "ctx"),
        P("ch", "ctx"),
        P("ch", "ctx"),
        P("ch", "ctx"),
        P(None, "ch", "ctx"),
        P("ch", None),
    )
    out_specs = (P("ch", "ctx"), P("ch", "ctx"), P("ch", "ctx"), P("ch", "ctx"), P(None, "ctx"))
    return jax.shard_map(shards, mesh=mesh, in_specs=in_specs, out_specs=out_specs, check_vma=False)
```

time: 155 us -> 109 us (0.70)
  Pallas kernels: 82.9 us -> 37 us
    pallas_call x1, Pallas kernels: 71.4 us -> 25 us  [shards(): pl.pallas_call(functools.partial(conv_kernel, width=width, halo=halo, fir...]
  transfers between devices with their start and end apart: 10 -> 10, of which waited for: 6 -> 6; matrix products, arithmetic and copies ran while one was open for 2% -> 3% of each run, Pallas kernels for 4% -> 6%
where the time goes in v1:
time: 109 us; the launch traced here: 108 us
  Pallas kernels  37 us (34%)
  waiting for transfers between devices  33.3 us (31%)
  starting transfers between devices  26.9 us (25%)
  local copies, waits for them, and re-layouts  7.8 us (7%)
  other arithmetic  2.05 us (2%)
    ppermute x8, waiting for transfers between devices, shift_by(): lax.ppermute(shard, axis, [(i, (i + by) % devices) for i in range(devices)])  27.4 us
    pallas_call x1, Pallas kernels, shards(): pl.pallas_call(functools.partial(conv_kernel, width=width, halo=halo, fir...  25 us
    ppermute x8, starting transfers between devices, shift_by(): lax.ppermute(shard, axis, [(i, (i + by) % devices) for i in range(devices)])  15.7 us
    all_to_all x1, starting transfers between devices, shards(): lax.all_to_all(jnp.broadcast_to(peak, (ch, 8, TILE)), 'ch', split_axis=0,...  7.66 us
    pallas_call x1, Pallas kernels, shards(): pl.pallas_call(scale_kernel, grid=steps, in_specs=[scalars, whole] + [til...  6.01 us
    pallas_call x1, Pallas kernels, shards(): pl.pallas_call(gate_kernel, grid=steps, in_specs=[scalars] + [tile] * 4,...  5.99 us
    all_to_all x1, waiting for transfers between devices, shards(): lax.all_to_all(jnp.broadcast_to(peak, (ch, 8, TILE)), 'ch', split_axis=0,...  5.47 us
    all_to_all x1, starting transfers between devices, shards(): lax.all_to_all(lag.reshape(groups, ctx, taps // ctx).transpose(1, 0, 2),...  3.53 us
  transfers between devices with their start and end apart: 10, of which 6 were waited for; matrix products, arithmetic and copies ran while one was open for 3% of the time, Pallas kernels for 6%

profile of v1, /device:TPU:0, one launch (start us, length us, event | category | flops | bytes accessed | tf_op | source)
XLA Modules:
  0.0 107.7 jit_solution(13856052585109600596)
XLA Ops:
  0.6 1.4 %copy.20.e_ref = s32[3,8,2]{2,1,0:T(8,128)} copy(s32[3,8,2]{1,2,0:T(2,128)} %param.10) | data formatting | bytes 384 | tf_op args[4]
  2.0 6.0 %gate.1 = (bf16[1024,256]{1,0:T(8,128)(2,1)}, bf16[1024,256]{1,0:T(8,128)(2,1)}) custom-call(s32[3,8,2]{2,1,0:T(8,128)} %copy.20.e_ref, bf16[1024,256]{1,0:T(8,128)(2,1)} %q_ref.1, bf16[1024,256]{1,0:T(8,128)(2,1)} %k_ref.3, bf16[1024,256]{1,0:T(8,128)(2,1)} %v_ref.3, bf16[1024,256]{1,0:T(8,128)(2,1)} %g_ref.3), custom_call_target="tpu_custom_call" | custom-call | tf_op jit(solution)/shard_map/gate/pallas_call | solution.py:195
  8.0 0.0 collective-permute-start
  8.0 4.0 %collective-permute-start.4 = (bf16[1024,256]{1,0:T(8,128)(2,1)}, bf16[1024,256]{1,0:T(8,128)(2,1)S(1)}, u32[]{:S(2)}, u32[]{:S(2)}) collective-permute-start(bf16[1024,256]{1,0:T(8,128)(2,1)} %get-tuple-element.15.refs_5_), channel_id=1, source_target_pairs={{0,120},{8,0},{16,8},{24,16},{32,24},{40,32},{48,40},{56,48},{64,5... | collective-permute-start | bytes 1572872 | tf_op jit(solution)/shard_map/ppermute | solution.py:19
  12.0 7.0 %collective-permute-done.refs_1_ = bf16[1024,256]{1,0:T(8,128)(2,1)S(1)} collective-permute-done((bf16[1024,256]{1,0:T(8,128)(2,1)}, bf16[1024,256]{1,0:T(8,128)(2,1)S(1)}, u32[]{:S(2)}, u32[]{:S(2)}) %collective-permute-start) | collective-permute-done | bytes 524320 | tf_op jit(solution)/shard_map/ppermute | solution.py:19
  19.0 0.0 copy-start
  19.0 0.0 collective-permute-start.1
  19.0 0.0 collective-permute-done.4.refs_6_
  19.0 0.0 copy-start.1
  19.0 3.9 %collective-permute-start.5 = (bf16[1024,256]{1,0:T(8,128)(2,1)S(1)}, bf16[1024,256]{1,0:T(8,128)(2,1)S(1)}, u32[]{:S(2)}, u32[]{:S(2)}) collective-permute-start(bf16[1024,256]{1,0:T(8,128)(2,1)S(1)} %collective-permute-done.4.refs_6_), channel_id=1, source_target_pairs={{0,120},{8,0},{16,8},{24,16},{32,24},{40,32},{48,40},{56,48},{64,5... | collective-permute-start | bytes 1572872 | tf_op jit(solution)/shard_map/ppermute | solution.py:19
  22.9 6.8 %collective-permute-done.1.refs_2_ = bf16[1024,256]{1,0:T(8,128)(2,1)S(1)} collective-permute-done((bf16[1024,256]{1,0:T(8,128)(2,1)S(1)}, bf16[1024,256]{1,0:T(8,128)(2,1)S(1)}, u32[]{:S(2)}, u32[]{:S(2)}) %collective-permute-start.1) | collective-permute-done | bytes 524320 | tf_op jit(solution)/shard_map/ppermute | solution.py:19
  29.7 0.0 copy-start.2
  29.7 0.0 collective-permute-start.2
  29.7 0.0 collective-permute-done.5.refs_7_
  29.7 0.0 copy-start.3
  29.7 3.9 %collective-permute-start.6 = (bf16[1024,256]{1,0:T(8,128)(2,1)S(1)}, bf16[1024,256]{1,0:T(8,128)(2,1)S(1)}, u32[]{:S(2)}, u32[]{:S(2)}) collective-permute-start(bf16[1024,256]{1,0:T(8,128)(2,1)S(1)} %collective-permute-done.5.refs_7_), channel_id=1, source_target_pairs={{0,120},{8,0},{16,8},{24,16},{32,24},{40,32},{48,40},{56,48},{64,5... | collective-permute-start | bytes 1572872 | tf_op jit(solution)/shard_map/ppermute | solution.py:19
  33.6 6.8 %collective-permute-done.2.refs_3_ = bf16[1024,256]{1,0:T(8,128)(2,1)S(1)} collective-permute-done((bf16[1024,256]{1,0:T(8,128)(2,1)S(1)}, bf16[1024,256]{1,0:T(8,128)(2,1)S(1)}, u32[]{:S(2)}, u32[]{:S(2)}) %collective-permute-start.2) | collective-permute-done | bytes 524320 | tf_op jit(solution)/shard_map/ppermute | solution.py:19
  40.4 0.0 copy-start.4
  40.4 0.0 collective-permute-start.3
  40.4 0.0 collective-permute-done.6.refs_8_
  40.4 0.0 copy-start.5
  40.4 3.9 %collective-permute-start.7 = (bf16[1024,256]{1,0:T(8,128)(2,1)S(1)}, bf16[1024,256]{1,0:T(8,128)(2,1)}, u32[]{:S(2)}, u32[]{:S(2)}) collective-permute-start(bf16[1024,256]{1,0:T(8,128)(2,1)S(1)} %collective-permute-done.6.refs_8_), channel_id=1, source_target_pairs={{0,120},{8,0},{16,8},{24,16},{32,24},{40,32},{48,40},{56,48},{64,5... | collective-permute-start | bytes 1572872 | tf_op jit(solution)/shard_map/ppermute | solution.py:19
  44.3 6.8 %collective-permute-done.3.refs_4_ = bf16[1024,256]{1,0:T(8,128)(2,1)S(1)} collective-permute-done((bf16[1024,256]{1,0:T(8,128)(2,1)S(1)}, bf16[1024,256]{1,0:T(8,128)(2,1)S(1)}, u32[]{:S(2)}, u32[]{:S(2)}) %collective-permute-start.3) | collective-permute-done | bytes 524320 | tf_op jit(solution)/shard_map/ppermute | solution.py:19
  51.1 0.0 copy-start.6
  51.1 0.8 copy-done.6
  51.9 0.0 collective-permute-done.7.refs_9_
  51.9 0.0 copy-done
  51.9 0.0 copy-done.1
  51.9 0.0 copy-done.2
  51.9 0.0 copy-done.3
  52.0 0.0 copy-done.4
  52.0 0.0 copy-done.5
  52.0 25.0 %conv.1 = (f32[1024,256]{1,0:T(8,128)}, f32[1024,256]{1,0:T(8,128)}, f32[64,1024]{1,0:T(8,128)}, f32[8,128]{1,0:T(8,128)}) custom-call(s32[3,8,2]{2,1,0:T(8,128)} %copy.20.e_ref, f32[64,1024]{1,0:T(8,128)} %taps_ref.1, bf16[1024,256]{1,0:T(8,128)(2,1)} %get-tuple-element.14.refs_0_, bf16[1024,256]{1,0:T(8,128)(2,1)} %copy-done, bf16[1024,256]{1,0:T(8,128)(2,1)} %copy-done.2, ...), custom_call_target="tpu_custom_call" | custom-call | tf_op jit(solution)/shard_map/conv/pallas_call | solution.py:212
  77.0 1.3 %broadcast_in_dim.4 = f32[8,8,128]{2,1,0:T(8,128)} broadcast(f32[8,128]{1,0:T(8,128)} %get-tuple-element.16), dimensions={1,2} | broadcast | bytes 36864 | tf_op jit(solution)/shard_map/broadcast_in_dim | solution.py:233
  78.3 7.7 %all-to-all-start = ((f32[8,8,128]{2,1,0:T(8,128)}), f32[8,8,128]{2,1,0:T(8,128)S(1)}, u32[]{:S(2)}, u32[]{:S(2)}) async-start(f32[8,8,128]{2,1,0:T(8,128)} %broadcast_in_dim.4), calls=%async_computation | async-start | bytes 65536 | tf_op jit(solution)/shard_map/all_to_all | solution.py:232
  85.9 1.1 %reshape.15 = f32[64,16,64]{2,1,0:T(8,128)S(1)} reshape(f32[64,1024]{1,0:T(8,128)} %get-tuple-element.22) | data formatting | bytes 524288 | tf_op jit(solution)/shard_map/reshape | solution.py:248
  87.0 0.2 copy.23
  87.2 1.0 reshape.16
  88.2 5.5 %all-to-all-done = f32[8,8,128]{2,1,0:T(8,128)S(1)} async-done(((f32[8,8,128]{2,1,0:T(8,128)}), f32[8,8,128]{2,1,0:T(8,128)S(1)}, u32[]{:S(2)}, u32[]{:S(2)}) %all-to-all-start) | async-done | bytes 32800 | tf_op jit(solution)/shard_map/all_to_all | solution.py:232
  93.7 3.5 %all-to-all-start.1 = ((f32[16,1,4096]{2,1,0:T(1,128)}), f32[16,1,4096]{2,1,0:T(1,128)S(1)}, u32[]{:S(2)}, u32[]{:S(2)}) async-start(f32[16,1,4096]{2,1,0:T(1,128)} %reshape.16), calls=%async_computation.1 | async-start | bytes 524288 | tf_op jit(solution)/shard_map/all_to_all | solution.py:247
  97.2 0.1 reduce_max.9
  97.3 0.1 slice.6
  97.4 0.7 broadcast_in_dim.10.peak_ref
  98.1 6.0 %scale.1 = (bf16[1024,256]{1,0:T(8,128)(2,1)}, bf16[1024,256]{1,0:T(8,128)(2,1)}, bf16[1024,256]{1,0:T(8,128)(2,1)}) custom-call(s32[3,8,2]{2,1,0:T(8,128)} %copy.20.e_ref, f32[8,128]{1,0:T(8,128)} %broadcast_in_dim.10.peak_ref, bf16[1024,256]{1,0:T(8,128)(2,1)} %k_ref.3, bf16[1024,256]{1,0:T(8,128)(2,1)} %v_ref.3, bf16[1024,256]{1,0:T(8,128)(2,1)} %g_ref.3, ...), custom_call_target="tpu_custom_call" | custom-call | tf_op jit(solution)/shard_map/scale/pallas_call | solution.py:237
  104.1 0.6 slice_bitcast_fusion
  104.7 0.4 all-to-all-done.1
  105.1 0.5 broadcast.2
  105.6 1.3 %reduce = f32[16,4096]{1,0:T(8,128)S(1)} reduce(f32[16,1,4096]{2,1,0:T(1,128)S(1)} %all-to-all-done.1, f32[]{:T(128)} %broadcast.2), dimensions={1}, to_apply=%all_to_all.7.reduce_sub_computation | reduce | bytes 524292 | tf_op jit(solution)/shard_map/all_to_all | solution.py:247
  106.8 0.2 reshape.17
  107.1 0.7 reduce_sum.9
Async XLA Ops:
  8.0 11.0 %collective-permute-start = (bf16[1024,256]{1,0:T(8,128)(2,1)}, bf16[1024,256]{1,0:T(8,128)(2,1)S(1)}, u32[]{:S(2)}, u32[]{:S(2)}) collective-permute-start(bf16[1024,256]{1,0:T(8,128)(2,1)} %get-tuple-element.14.refs_0_), channel_id=1, source_target_pairs={{0,8},{8,16},{16,24},{24,32},{32,40},{40,48},{48,56},{56,64},{64,7... | collective-permute-start | bytes 1572872 | tf_op jit(solution)/shard_map/ppermute | solution.py:19
  8.0 11.0 %collective-permute-start.4 = (bf16[1024,256]{1,0:T(8,128)(2,1)}, bf16[1024,256]{1,0:T(8,128)(2,1)S(1)}, u32[]{:S(2)}, u32[]{:S(2)}) collective-permute-start(bf16[1024,256]{1,0:T(8,128)(2,1)} %get-tuple-element.15.refs_5_), channel_id=1, source_target_pairs={{0,120},{8,0},{16,8},{24,16},{32,24},{40,32},{48,40},{56,48},{64,5... | collective-permute-start | bytes 1572872 | tf_op jit(solution)/shard_map/ppermute | solution.py:19
  19.0 33.0 %copy-start = (bf16[1024,256]{1,0:T(8,128)(2,1)}, bf16[1024,256]{1,0:T(8,128)(2,1)S(1)}, u32[]{:S(2)}) copy-start(bf16[1024,256]{1,0:T(8,128)(2,1)S(1)} %collective-permute-done.refs_1_) | copy-start | bytes 1572868
  19.0 10.7 %collective-permute-start.1 = (bf16[1024,256]{1,0:T(8,128)(2,1)S(1)}, bf16[1024,256]{1,0:T(8,128)(2,1)S(1)}, u32[]{:S(2)}, u32[]{:S(2)}) collective-permute-start(bf16[1024,256]{1,0:T(8,128)(2,1)S(1)} %collective-permute-done.refs_1_), channel_id=1, source_target_pairs={{0,8},{8,16},{16,24},{24,32},{32,40},{40,48},{48,56},{56,64},{64,7... | collective-permute-start | bytes 1572872 | tf_op jit(solution)/shard_map/ppermute | solution.py:19
  19.0 33.0 %copy-start.1 = (bf16[1024,256]{1,0:T(8,128)(2,1)}, bf16[1024,256]{1,0:T(8,128)(2,1)S(1)}, u32[]{:S(2)}) copy-start(bf16[1024,256]{1,0:T(8,128)(2,1)S(1)} %collective-permute-done.4.refs_6_) | copy-start | bytes 1572868
  19.0 10.7 %collective-permute-start.5 = (bf16[1024,256]{1,0:T(8,128)(2,1)S(1)}, bf16[1024,256]{1,0:T(8,128)(2,1)S(1)}, u32[]{:S(2)}, u32[]{:S(2)}) collective-permute-start(bf16[1024,256]{1,0:T(8,128)(2,1)S(1)} %collective-permute-done.4.refs_6_), channel_id=1, source_target_pairs={{0,120},{8,0},{16,8},{24,16},{32,24},{40,32},{48,40},{56,48},{64,5... | collective-permute-start | bytes 1572872 | tf_op jit(solution)/shard_map/ppermute | solution.py:19
  29.7 22.3 %copy-start.2 = (bf16[1024,256]{1,0:T(8,128)(2,1)}, bf16[1024,256]{1,0:T(8,128)(2,1)S(1)}, u32[]{:S(2)}) copy-start(bf16[1024,256]{1,0:T(8,128)(2,1)S(1)} %collective-permute-done.1.refs_2_) | copy-start | bytes 1572868
  29.7 10.7 %collective-permute-start.2 = (bf16[1024,256]{1,0:T(8,128)(2,1)S(1)}, bf16[1024,256]{1,0:T(8,128)(2,1)S(1)}, u32[]{:S(2)}, u32[]{:S(2)}) collective-permute-start(bf16[1024,256]{1,0:T(8,128)(2,1)S(1)} %collective-permute-done.1.refs_2_), channel_id=1, source_target_pairs={{0,8},{8,16},{16,24},{24,32},{32,40},{40,48},{48,56},{56,64},{64,7... | collective-permute-start | bytes 1572872 | tf_op jit(solution)/shard_map/ppermute | solution.py:19
  29.7 22.3 %copy-start.3 = (bf16[1024,256]{1,0:T(8,128)(2,1)}, bf16[1024,256]{1,0:T(8,128)(2,1)S(1)}, u32[]{:S(2)}) copy-start(bf16[1024,256]{1,0:T(8,128)(2,1)S(1)} %collective-permute-done.5.refs_7_) | copy-start | bytes 1572868
  29.7 10.7 %collective-permute-start.6 = (bf16[1024,256]{1,0:T(8,128)(2,1)S(1)}, bf16[1024,256]{1,0:T(8,128)(2,1)S(1)}, u32[]{:S(2)}, u32[]{:S(2)}) collective-permute-start(bf16[1024,256]{1,0:T(8,128)(2,1)S(1)} %collective-permute-done.5.refs_7_), channel_id=1, source_target_pairs={{0,120},{8,0},{16,8},{24,16},{32,24},{40,32},{48,40},{56,48},{64,5... | collective-permute-start | bytes 1572872 | tf_op jit(solution)/shard_map/ppermute | solution.py:19
  40.4 11.6 %copy-start.4 = (bf16[1024,256]{1,0:T(8,128)(2,1)}, bf16[1024,256]{1,0:T(8,128)(2,1)S(1)}, u32[]{:S(2)}) copy-start(bf16[1024,256]{1,0:T(8,128)(2,1)S(1)} %collective-permute-done.2.refs_3_) | copy-start | bytes 1572868
  40.4 10.7 %collective-permute-start.3 = (bf16[1024,256]{1,0:T(8,128)(2,1)S(1)}, bf16[1024,256]{1,0:T(8,128)(2,1)S(1)}, u32[]{:S(2)}, u32[]{:S(2)}) collective-permute-start(bf16[1024,256]{1,0:T(8,128)(2,1)S(1)} %collective-permute-done.2.refs_3_), channel_id=1, source_target_pairs={{0,8},{8,16},{16,24},{24,32},{32,40},{40,48},{48,56},{56,64},{64,7... | collective-permute-start | bytes 1572872 | tf_op jit(solution)/shard_map/ppermute | solution.py:19
  40.4 11.6 %copy-start.5 = (bf16[1024,256]{1,0:T(8,128)(2,1)}, bf16[1024,256]{1,0:T(8,128)(2,1)S(1)}, u32[]{:S(2)}) copy-start(bf16[1024,256]{1,0:T(8,128)(2,1)S(1)} %collective-permute-done.6.refs_8_) | copy-start | bytes 1572868
  40.4 11.5 %collective-permute-start.7 = (bf16[1024,256]{1,0:T(8,128)(2,1)S(1)}, bf16[1024,256]{1,0:T(8,128)(2,1)}, u32[]{:S(2)}, u32[]{:S(2)}) collective-permute-start(bf16[1024,256]{1,0:T(8,128)(2,1)S(1)} %collective-permute-done.6.refs_8_), channel_id=1, source_target_pairs={{0,120},{8,0},{16,8},{24,16},{32,24},{40,32},{48,40},{56,48},{64,5... | collective-permute-start | bytes 1572872 | tf_op jit(solution)/shard_map/ppermute | solution.py:19
  51.1 0.8 copy-start.6
  78.3 15.4 %all-to-all-start = ((f32[8,8,128]{2,1,0:T(8,128)}), f32[8,8,128]{2,1,0:T(8,128)S(1)}, u32[]{:S(2)}, u32[]{:S(2)}) async-start(f32[8,8,128]{2,1,0:T(8,128)} %broadcast_in_dim.4), calls=%async_computation | async-start | bytes 65536 | tf_op jit(solution)/shard_map/all_to_all | solution.py:232
  93.7 11.4 %all-to-all-start.1 = ((f32[16,1,4096]{2,1,0:T(1,128)}), f32[16,1,4096]{2,1,0:T(1,128)S(1)}, u32[]{:S(2)}, u32[]{:S(2)}) async-start(f32[16,1,4096]{2,1,0:T(1,128)} %reshape.16), calls=%async_computation.1 | async-start | bytes 524288 | tf_op jit(solution)/shard_map/all_to_all | solution.py:247
